TPU v7x, 32 devices: a whole 2x2x4 slice. The times are simulated.
32 devices in a mesh: row: 4 (over z), col: 8 (over y, x, core).
Axes of the slice: x: 2, y: 2, z: 4, core: 2. Of those that a mesh axis runs over, the one named last changes fastest.
Arguments:
- splat_params: float32 [10, 2097152], P(None, ('row', 'col')), as said below
- list_owner: int32 [128, 1024, 1], P(('row', 'col')), may hold values from 0 to 31; in each aligned block of 4096 rows (0 to 4095, 4096 to 8191, ..., all dimensions but the last counted through in order) at most 256 rows name the same one
- list_slot: int32 [128, 1024], P(('row', 'col')), may hold values from 0 to 65535
- list_length: int32 [128], P(('row', 'col')), may hold values from 512 to 1024, as said below
- target: float32 [4, 128, 256], P(None, ('row', 'col')), may hold values from 0 to 1
Outputs:
- rendered: float32 [4, 128, 256], P(None, ('row', 'col'))
- splat_grads: float32 [10, 2097152], P(None, ('row', 'col'))
Inputs may be any that keep to these rules, and one draw needn't show every extreme that they name: `list_owner`: within the entries of one device's tiles (aligned blocks of 4096 entries), no owner is named more than 256 times, a bound that some block reaches. `list_length`: some tile has exactly 1024 live entries; every tile has at least 512. `splat_params`: conic entries satisfy a > 0, c > 0 and b * b < a * c; opacity lies in (0, 0.02]; colours and depth lie in [0, 1].
All inputs are finite; a program needn't handle non-finite values.
Results may differ from a plain program's by a relative error of at most 0.0003.
Values sent between devices are 32-bit elements; how exact they have to be, the bound alone decides.
A program may use at most 128 MiB of HBM per device.

v0:
```python
import jax
import jax.numpy as jnp
from jax import lax
from jax.sharding import PartitionSpec as P

SIDE = 16
SB = 256


precise = lax.Precision.HIGHEST


def render_tile(values, tile_target):
    pixel_count = tile_target.shape[1]
    pixel_index = jnp.arange(pixel_count)
    pixel_x = (pixel_index % SIDE).astype(jnp.float32) + 0.5
    pixel_y = (pixel_index // SIDE).astype(jnp.float32) + 0.5
    live_count = jnp.sum((values[5] > 0.0).astype(jnp.int32))
    blocks = (live_count + SB - 1) // SB
    block_index = jnp.arange(SB)
    strict = (block_index[:, None] < block_index[None, :]).astype(jnp.float32)
    inclusive = (block_index[:, None] <= block_index[None, :]).astype(jnp.float32)

    def geometry(start):
        block_values = lax.dynamic_slice_in_dim(values, start, SB, 1)
        offset_x = pixel_x[:, None] - block_values[0][None, :]
        offset_y = pixel_y[:, None] - block_values[1][None, :]
        exponent = (
            0.5 * (block_values[2] * offset_x * offset_x + block_values[4] * offset_y * offset_y)
            + block_values[3] * offset_x * offset_y
        )
        falloff = jnp.exp(-exponent)
        alphas = block_values[5][None, :] * falloff
        log_keep = jnp.log1p(-alphas)
        return (block_values, offset_x, offset_y, falloff, alphas, log_keep)

    def forward(block_step, state):
        carried, rendered = state
        block_values, offset_x, offset_y, falloff, alphas, log_keep = geometry(block_step * SB)
        transmit = jnp.exp(carried[:, None] + jnp.dot(log_keep, strict, precision=precise))
        weight = alphas * transmit
        rendered = rendered + lax.dot_general(
            block_values[6:10], weight, (((1,), (1,)), ((), ())), precision=precise
        )
        return (carried + jnp.sum(log_keep, axis=1), rendered)

    start_state = (jnp.zeros((pixel_count,), jnp.float32), jnp.zeros((4, pixel_count), jnp.float32))
    carried, rendered = lax.fori_loop(0, blocks, forward, start_state)
    grad_image = 2.0 * (rendered - tile_target)
    grand_total = jnp.sum(grad_image * rendered, axis=0)

    def backward(block_step, state):
        carried, spent_before, grad_rows = state
        start = block_step * SB
        block_values, offset_x, offset_y, falloff, alphas, log_keep = geometry(start)
        transmit = jnp.exp(carried[:, None] + jnp.dot(log_keep, strict, precision=precise))
        weight = alphas * transmit
        shading = lax.dot_general(
            grad_image, block_values[6:10], (((0,), (0,)), ((), ())), precision=precise
        )
        spent_sum = weight * shading
        before = spent_before[:, None] + jnp.dot(spent_sum, inclusive, precision=precise)
        grad_alpha = transmit * shading - (grand_total[:, None] - before) / (1.0 - alphas)
        grad_power = -grad_alpha * alphas
        conic_a = block_values[2]
        conic_b = block_values[3]
        conic_c = block_values[4]
        grad_mean_x = jnp.sum(-grad_power * (conic_a * offset_x + conic_b * offset_y), axis=0)
        grad_mean_y = jnp.sum(-grad_power * (conic_c * offset_y + conic_b * offset_x), axis=0)
        grad_a = jnp.sum(grad_power * 0.5 * offset_x * offset_x, axis=0)
        grad_b = jnp.sum(grad_power * offset_x * offset_y, axis=0)
        grad_c = jnp.sum(grad_power * 0.5 * offset_y * offset_y, axis=0)
        live_mask = (block_values[5] > 0.0).astype(jnp.float32)
        grad_opacity = jnp.sum(grad_alpha * falloff, axis=0) * live_mask
        grad_colours = jnp.dot(grad_image, weight, precision=precise)
        geometry_grads = jnp.stack([grad_mean_x, grad_mean_y, grad_a, grad_b, grad_c, grad_opacity])
        update = jnp.concatenate([geometry_grads, grad_colours], axis=0)
        grad_rows = lax.dynamic_update_slice_in_dim(grad_rows, update, start, 1)
        return (
            carried + jnp.sum(log_keep, axis=1),
            spent_before + jnp.sum(spent_sum, axis=1),
            grad_rows,
        )

    back_state = (
        jnp.zeros((pixel_count,), jnp.float32),
        jnp.zeros((pixel_count,), jnp.float32),
        jnp.zeros(values.shape, jnp.float32),
    )
    finished = lax.fori_loop(0, blocks, backward, back_state)
    return (rendered, finished[2])


def render_all(values, tile_targets):
    tile_count = values.shape[1]

    def render_one(tile_step, state):
        images, grad_rows = state
        tile_values = lax.dynamic_index_in_dim(values, tile_step, 1, keepdims=False)
        tile_target = lax.dynamic_index_in_dim(tile_targets, tile_step, 1, keepdims=False)
        rendered, tile_grads = render_tile(tile_values, tile_target)
        images = lax.dynamic_update_index_in_dim(images, rendered, tile_step, 1)
        grad_rows = lax.dynamic_update_index_in_dim(grad_rows, tile_grads, tile_step, 1)
        return (images, grad_rows)

    start_state = (jnp.zeros(tile_targets.shape, jnp.float32), jnp.zeros(values.shape, jnp.float32))
    return lax.fori_loop(0, tile_count, render_one, start_state)


def body(splat_params, list_owner, list_slot, list_length, target):
    devices = lax.axis_size(("row", "col"))
    tile_count = list_slot.shape[0]
    list_count = list_slot.shape[1]
    entries = tile_count * list_count
    capacity = 2 * entries // devices
    owners = list_owner.reshape(entries)
    slot_ids = list_slot.reshape(entries)
    sort_order = jnp.argsort(owners, stable=True)
    sorted_owner = owners[sort_order]
    starts = jnp.searchsorted(sorted_owner, jnp.arange(devices, dtype=jnp.int32))
    position = jnp.arange(entries, dtype=jnp.int32) - starts[sorted_owner]
    slot_rank = jnp.zeros((entries,), jnp.int32).at[sort_order].set(position)
    requests = jnp.zeros((devices, capacity), jnp.int32).at[owners, slot_rank].set(slot_ids)
    asked_slots = lax.all_to_all(requests, ("row", "col"), split_axis=0, concat_axis=0, tiled=True)
    looked = jnp.take(splat_params, asked_slots, axis=1)
    answer = lax.all_to_all(looked, ("row", "col"), split_axis=1, concat_axis=1, tiled=True)
    replies, asked_slots = (answer, asked_slots[None])
    fetched = replies[:, owners, slot_rank].reshape(10, tile_count, list_count)
    live_mask = (jnp.arange(list_count)[None, :] < list_length[:, None]).astype(jnp.float32)
    values = jnp.concatenate([fetched[:5], fetched[5:6] * live_mask[None], fetched[6:]], axis=0)
    images, entry_grads = render_all(values, target)
    flat_grads = entry_grads.reshape(10, entries)
    outgoing = (
        jnp.zeros((10, devices, capacity), jnp.float32).at[:, owners, slot_rank].set(flat_grads)
    )
    incoming = lax.all_to_all(outgoing, ("row", "col"), split_axis=1, concat_axis=1, tiled=True)
    splat_grads = jnp.zeros(splat_params.shape, jnp.float32).at[:, asked_slots[0]].add(incoming)
    return (images, splat_grads)


def solution(mesh):
    in_specs = (
        P(None, ("row", "col")),
        P(("row", "col"), None, None),
        P(("row", "col"), None),
        P(("row", "col")),
        P(None, ("row", "col"), None),
    )
    out_specs = (P(None, ("row", "col"), None), P(None, ("row", "col")))
    return jax.shard_map(body, mesh=mesh, in_specs=in_specs, out_specs=out_specs, check_vma=False)
```

profile of v0, /device:TPU:0, one launch (start us, length us, event | category | flops | bytes accessed | tf_op | source)
XLA Modules:
  0.0 435.0 jit_solution(15986858977022546127)
XLA Ops:
  0.7 6.5 %sort.17 = (s32[4096]{0:T(1024)}, s32[4096]{0:T(1024)S(1)}) sort(s32[4096]{0:T(1024)} %bitcast.156, s32[4096]{0:T(1024)S(1)} %iota.64), dimensions={0}, to_apply=%region_0.0 | sort | flops 49152 | bytes 65536 | tf_op jit(solution)/shard_map/jit(argsort)/sort | solution.py:118
  7.2 23.0 %gather_fusion.1 = s32[4096]{0:T(1024)S(1)} fusion(s32[4096]{0:T(1024)S(1)} %bitcast.157, s32[4096]{0:T(1024)S(1)} %get-tuple-element.561), kind=kCustom, calls=%fused_computation.1 | custom fusion | bytes 49152 | tf_op jit(solution)/shard_map/gather | solution.py:119
  30.3 9.8 %while.141 = (s32[]{:T(128)}, u32[32]{0:T(128)S(1)}, u32[32]{0:T(128)S(1)}, s32[4096]{0:T(1024)S(1)}, s32[]{:T(128)}, /*index=5*/s32[]{:T(128)}, s32[]{}) while((s32[]{:T(128)}, u32[32]{0:T(128)S(1)}, u32[32]{0:T(128)S(1)}, s32[4096]{0:T(1024)S(1)}, s32[]{:T(128)}, /*index=5*/s32[]{:T(128)}, s32[]{}) %tuple.220), condition=%wide.region_2.3_spmd.clone, body=%wide.region_1.2_spmd.clone.sunk | while | flops 1444 | bytes 5732 | solution.py:120
  47.1 15.9 %select_subtract_fusion = s32[4096]{0:T(1024)S(1)} fusion(pred[4096]{0:T(1024)(128)(4,1)S(1)} %get-tuple-element.492, pred[4096]{0:T(1024)(128)(4,1)S(1)} %get-tuple-element.491, pred[4096]{0:T(1024)(128)(4,1)S(1)} %get-tuple-element.490, pred[4096]{0:T(1024)(128)(4,1)S(1)} %get-tuple-element.489, pred[4096]{0:T(1024)(128)(4,1)S(1)} %get-tuple-element.488, ...), kind=kLoop, calls=%fused_computation.180 | loop fusion | flops 106496 | bytes 135268 | tf_op jit(solution)/shard_map/sub | solution.py:121
  63.0 15.5 %scatter_custom_fusion = s32[4096]{0:T(1024)S(1)} fusion(s32[4096]{0:T(1024)S(1)} %get-tuple-element.562, s32[4096]{0:T(1024)S(1)} %select_subtract_fusion, s32[]{:T(128)} %constant.288.clone.1), kind=kCustom, calls=%fused_computation.187 | custom fusion | bytes 16388 | tf_op jit(solution)/shard_map/scatter | solution.py:122
  78.9 16.1 %scatter_custom_fusion.2 = s32[8192]{0:T(1024)} fusion(s32[4096]{0:T(1024)S(1)} %broadcast_select_fusion.2, s32[4096]{0:T(1024)S(1)} %bitcast.216, s32[]{:T(128)} %constant.288.clone.1), kind=kCustom, calls=%fused_computation.181 | custom fusion | bytes 32772
  95.0 7.3 %all-to-all-start = ((s32[32,1,256]{2,1,0:T(1,128)}), s32[32,1,256]{2,1,0:T(1,128)S(1)}, u32[]{:S(2)}, u32[]{:S(2)}) async-start(s32[32,1,256]{2,1,0:T(1,128)} %bitcast.41), calls=%async_computation | async-start | bytes 65536 | tf_op jit(solution)/shard_map/all_to_all | solution.py:124
  102.3 16.9 %copy.35 = f32[10,65536]{0,1:T(8,128)} copy(f32[10,65536]{1,0:T(8,128)} %param.13) | data formatting | bytes 5242880 | tf_op args[0]
  119.3 38.5 %gather_fusion.2 = f32[8192,10]{1,0:T(8,128)} fusion(f32[10,65536]{0,1:T(8,128)} %copy.35, s32[8192]{0:T(1024)S(1)} %broadcast_clamp_fusion), kind=kCustom, calls=%fused_computation.2 | custom fusion | bytes 688128 | tf_op jit(solution)/shard_map/jit(_take)/gather | solution.py:125
  161.6 6.0 %all-to-all-start.1 = ((f32[10,32,256]{2,0,1:T(8,128)}), f32[10,32,256]{2,0,1:T(8,128)S(1)}, u32[]{:S(2)}, u32[]{:S(2)}) async-start(f32[10,32,256]{2,0,1:T(8,128)} %select_bitcast_fusion), calls=%async_computation.1 | async-start | bytes 1048576 | tf_op jit(solution)/shard_map/all_to_all | solution.py:126
  167.6 15.4 %all-to-all-done.1 = f32[10,32,256]{2,0,1:T(8,128)S(1)} async-done(((f32[10,32,256]{2,0,1:T(8,128)}), f32[10,32,256]{2,0,1:T(8,128)S(1)}, u32[]{:S(2)}, u32[]{:S(2)}) %all-to-all-start.1) | async-done | bytes 327712 | tf_op jit(solution)/shard_map/all_to_all | solution.py:126
  185.7 44.0 %gather_fusion.3 = f32[4096,10]{1,0:T(8,128)S(1)} fusion(f32[10,32,256]{0,2,1:T(8,128)} %copy.37, s32[4096]{0:T(1024)S(1)} %bitcast.160), kind=kCustom, calls=%fused_computation.3 | custom fusion | bytes 360448 | tf_op jit(solution)/shard_map/gather | solution.py:128
  235.8 63.0 %while.140 = (s32[]{:T(128)}, f32[4,4,256]{2,1,0:T(4,128)S(1)}, f32[10,4,1024]{2,1,0:T(4,128)S(1)}, f32[10,4,1024]{2,0,1:T(8,128)S(1)}, f32[4,4,256]{2,1,0:T(4,1...) while((s32[]{:T(128)}, f32[4,4,256]{2,1,0:T(4,128)S(1)}, ...), condition=%wide.region_21.22_spmd, body=%wide.region_5.21_spmd.sunk | while | flops 622607104 | bytes 2349421 | solution.py:107
  237.2 4.5 %while.142 = (s32[]{:T(128)}, f32[256]{0:T(256)S(1)}, f32[4,256]{1,0:T(4,128)S(1)}, s32[]{:T(128)}, f32[10,1024]{1,0:T(8,128)S(1)}, /*index=5*/s32[]{:T(128)}, s...) while((s32[]{:T(128)}, f32[256]{0:T(256)S(1)}, ...), condition=%wide.region_9.9_spmd.clone, body=%wide.region_7.8_spmd.clone.sunk | while | flops 207492112 | bytes 572707 | solution.py:48
  242.5 8.0 %while.143 = (s32[]{:T(128)}, f32[256]{0:T(256)S(1)}, f32[256]{0:T(256)S(1)}, f32[10,1024]{1,0:T(8,128)S(1)}, s32[]{:T(128)}, /*index=5*/f32[10,1024]{1,0:T(8,12...) while((s32[]{:T(128)}, f32[256]{0:T(256)S(1)}, ...), condition=%wide.region_20.20_spmd.clone, body=%wide.region_11.19_spmd.clone.sunk | while | flops 415108096 | bytes 1440063 | solution.py:90
  253.0 4.5 %while.142 = (s32[]{:T(128)}, f32[256]{0:T(256)S(1)}, f32[4,256]{1,0:T(4,128)S(1)}, s32[]{:T(128)}, f32[10,1024]{1,0:T(8,128)S(1)}, /*index=5*/s32[]{:T(128)}, s...) while((s32[]{:T(128)}, f32[256]{0:T(256)S(1)}, ...), condition=%wide.region_9.9_spmd.clone, body=%wide.region_7.8_spmd.clone.sunk | while | flops 207492112 | bytes 572707 | solution.py:48
  258.2 8.0 %while.143 = (s32[]{:T(128)}, f32[256]{0:T(256)S(1)}, f32[256]{0:T(256)S(1)}, f32[10,1024]{1,0:T(8,128)S(1)}, s32[]{:T(128)}, /*index=5*/f32[10,1024]{1,0:T(8,12...) while((s32[]{:T(128)}, f32[256]{0:T(256)S(1)}, ...), condition=%wide.region_20.20_spmd.clone, body=%wide.region_11.19_spmd.clone.sunk | while | flops 415108096 | bytes 1440063 | solution.py:90
  268.7 4.5 %while.142 = (s32[]{:T(128)}, f32[256]{0:T(256)S(1)}, f32[4,256]{1,0:T(4,128)S(1)}, s32[]{:T(128)}, f32[10,1024]{1,0:T(8,128)S(1)}, /*index=5*/s32[]{:T(128)}, s...) while((s32[]{:T(128)}, f32[256]{0:T(256)S(1)}, ...), condition=%wide.region_9.9_spmd.clone, body=%wide.region_7.8_spmd.clone.sunk | while | flops 207492112 | bytes 572707 | solution.py:48
  274.0 8.0 %while.143 = (s32[]{:T(128)}, f32[256]{0:T(256)S(1)}, f32[256]{0:T(256)S(1)}, f32[10,1024]{1,0:T(8,128)S(1)}, s32[]{:T(128)}, /*index=5*/f32[10,1024]{1,0:T(8,12...) while((s32[]{:T(128)}, f32[256]{0:T(256)S(1)}, ...), condition=%wide.region_20.20_spmd.clone, body=%wide.region_11.19_spmd.clone.sunk | while | flops 415108096 | bytes 1440063 | solution.py:90
  289.7 8.0 %while.143 = (s32[]{:T(128)}, f32[256]{0:T(256)S(1)}, f32[256]{0:T(256)S(1)}, f32[10,1024]{1,0:T(8,128)S(1)}, s32[]{:T(128)}, /*index=5*/f32[10,1024]{1,0:T(8,12...) while((s32[]{:T(128)}, f32[256]{0:T(256)S(1)}, ...), condition=%wide.region_20.20_spmd.clone, body=%wide.region_11.19_spmd.clone.sunk | while | flops 415108096 | bytes 1440063 | solution.py:90
  299.7 12.8 %scatter_custom_fusion.3 = f32[10,8192]{0,1:T(8,128)} fusion(s32[4096]{0:T(1024)S(1)} %broadcast_select_fusion.2, f32[4096,10]{1,0:T(8,128)S(1)} %copy.43, f32[]{:T(128)} %constant.289.clone.1), kind=kCustom, calls=%fused_computation.132 | custom fusion | bytes 327684
  315.4 33.6 %all_to_all.25 = f32[10,32,256]{2,0,1:T(8,128)S(1)} all-to-all(f32[10,32,256]{2,0,1:T(8,128)S(1)} %copy.44), channel_id=1, replica_groups=mesh['row'=4,'col'=8] {'row','col'}, dimensions={1} | all-to-all | bytes 655360 | tf_op jit(solution)/shard_map/all_to_all | solution.py:136
  351.7 63.9 %scatter_custom_fusion.1 = f32[10,65536]{0,1:T(8,128)} fusion(s32[8192]{0:T(1024)S(1)} %bitcast.213, f32[8192,10]{1,0:T(8,128)} %bitcast.169, f32[]{:T(128)} %constant.289.clone.1), kind=kCustom, calls=%fused_computation.129 | custom fusion | flops 81920 | bytes 2621952 | tf_op jit(solution)/shard_map/scatter-add | solution.py:137
  415.6 19.4 %copy.48 = f32[10,65536]{1,0:T(8,128)} copy(f32[10,65536]{0,1:T(8,128)} %scatter_custom_fusion.1) | data formatting | bytes 5242880
  (358 shorter events, 98.8 us)
Async XLA Ops:
  0.6 6.6 %copy-start = (s32[4,1024,1]{1,2,0:T(1,128)S(1)}, s32[4,1024,1]{1,2,0:T(1,128)}, u32[]{:S(2)}) copy-start(s32[4,1024,1]{1,2,0:T(1,128)} %param.14) | copy-start | bytes 49156
  7.2 71.4 %copy-start.4 = (s32[2]{0:T(128)S(1)}, s32[2]{0:T(128)}, u32[]{:S(2)}) copy-start(s32[2]{0:T(128)} %constant.302) | copy-start | bytes 28
  7.2 71.5 %copy-start.3 = (s32[2]{0:T(128)S(1)}, s32[2]{0:T(128)}, u32[]{:S(2)}) copy-start(s32[2]{0:T(128)} %constant.305) | copy-start | bytes 28
  7.2 71.6 %copy-start.1 = (s32[4,1024]{1,0:T(4,128)S(1)}, s32[4,1024]{1,0:T(4,128)}, u32[]{:S(2)}) copy-start(s32[4,1024]{1,0:T(4,128)} %param.15) | copy-start | bytes 49156
  95.0 24.3 %all-to-all-start = ((s32[32,1,256]{2,1,0:T(1,128)}), s32[32,1,256]{2,1,0:T(1,128)S(1)}, u32[]{:S(2)}, u32[]{:S(2)}) async-start(s32[32,1,256]{2,1,0:T(1,128)} %bitcast.41), calls=%async_computation | async-start | bytes 65536 | tf_op jit(solution)/shard_map/all_to_all | solution.py:124
  161.6 21.5 %all-to-all-start.1 = ((f32[10,32,256]{2,0,1:T(8,128)}), f32[10,32,256]{2,0,1:T(8,128)S(1)}, u32[]{:S(2)}, u32[]{:S(2)}) async-start(f32[10,32,256]{2,0,1:T(8,128)} %select_bitcast_fusion), calls=%async_computation.1 | async-start | bytes 1048576 | tf_op jit(solution)/shard_map/all_to_all | solution.py:126
  231.6 4.0 copy-start.2
  298.9 16.6 %copy-start.5 = (f32[4,4,256]{2,1,0:T(4,128)}, f32[4,4,256]{2,1,0:T(4,128)S(1)}, u32[]{:S(2)}) copy-start(f32[4,4,256]{2,1,0:T(4,128)S(1)} %get-tuple-element.458) | copy-start | bytes 49156
where the time goes:
time: 440 us; the launch traced here: 435 us
  local copies, waits for them, and re-layouts  226 us (51%)
  other arithmetic  102 us (23%)
  matrix products  38.7 us (9%)
  blocking collectives  33.6 us (8%)
  waiting for transfers between devices  15.4 us (4%)
  starting transfers between devices  13.3 us (3%)
  loops' own time  4.77 us (1%)
    unnamed x19, local copies, waits for them, and re-layouts  65.5 us
    scatter-add x1, other arithmetic, body(): jnp.zeros(splat_params.shape, jnp.float32).at[:, asked_slots[0]]  63.9 us
    gather x1, local copies, waits for them, and re-layouts, body(): fetched = replies[:, owners, slot_rank].reshape(10, tile_count, list_count)  44 us
    gather x2, local copies, waits for them, and re-layouts, body(): looked = jnp.take(splat_params, asked_slots, axis=1)  41.3 us
    all_to_all x1, blocking collectives, body(): lax.all_to_all(outgoing, ('row', 'col'), split_axis=1, concat_axis=1, til...  33.6 us
    gather x1, local copies, waits for them, and re-layouts, body(): sorted_owner = owners[sort_order]  23 us
    sub x1, other arithmetic, body(): position = jnp.arange(entries, dtype=jnp.int32) - starts[sorted_owner]  15.9 us
    scatter x1, local copies, waits for them, and re-layouts, body(): slot_rank = jnp.zeros((entries,), jnp.int32).at[sort_order].set(position)  15.5 us
  transfers between devices with their start and end apart: 2, of which 1 were waited for; matrix products, arithmetic and copies ran while one was open for 4% of the time, Pallas kernels for 0%

commit v1 on v0

v1 whole, which is shorter than its diff:
```python
import functools

import jax
import jax.numpy as jnp
from jax import lax
from jax.experimental import pallas as pl
from jax.experimental.pallas import tpu as pltpu
from jax.sharding import PartitionSpec as P

SIDE = 16
SB = 256
LANES = 256
CH = 10
F32 = jnp.float32
BF16 = jnp.bfloat16
NT = (((1,), (1,)), ((), ()))


def iota(shape, dim):
    return lax.broadcasted_iota(jnp.int32, shape, dim)


def split(x):
    high = x.astype(BF16)
    return high, (x - high.astype(F32)).astype(BF16)


def mm(a, b):
    return jnp.dot(a, b, preferred_element_type=F32)


def mm_nt(a, b):
    return lax.dot_general(a, b, NT, preferred_element_type=F32)


def one_hot(index, size):
    return jnp.where(iota((size, index.shape[1]), 0) == index, 1.0, 0.0).astype(BF16)


def plan_kernel(own_ref, slot_ref, req_ref, rank_ref):
    devices, cap = req_ref.shape
    entries = own_ref.shape[1]
    strict = jnp.where(iota((SB, SB), 0) < iota((SB, SB), 1), 1.0, 0.0).astype(BF16)
    carry = jnp.zeros((devices, 1), F32)
    high = jnp.zeros((devices, cap), F32)
    low = jnp.zeros((devices, cap), F32)
    for j in range(entries // SB):
        part = slice(j * SB, (j + 1) * SB)
        mine = iota((devices, SB), 0) == own_ref[:, part]
        ones = jnp.where(mine, 1.0, 0.0)
        count = mm(ones.astype(BF16), strict) + carry
        rank = jnp.sum(ones * count, axis=0, keepdims=True).astype(jnp.int32)
        carry = carry + jnp.sum(ones, axis=1, keepdims=True)
        rank_ref[:, part] = rank
        slots = slot_ref[:, part]
        places = one_hot(rank, cap)
        slot_high = (slots >> 8).astype(F32)
        slot_low = (slots & 255).astype(F32)
        high = high + mm_nt(jnp.where(mine, slot_high, 0.0).astype(BF16), places)
        low = low + mm_nt(jnp.where(mine, slot_low, 0.0).astype(BF16), places)
    req_ref[...] = (high * 256.0 + low).astype(jnp.int32)


def gather_kernel(ask_ref, table_ref, out_ref, high_ref, low_ref):
    width = table_ref.shape[1]
    rows = table_ref.shape[0] // CH

    @pl.when(pl.program_id(0) == 0)
    def _():
        for ch in range(CH):
            part = slice(ch * rows, (ch + 1) * rows)
            high, low = split(table_ref[part, :])
            high_ref[part, :] = high
            low_ref[part, :] = low

    index = ask_ref[0]
    column = one_hot(index & (width - 1), width)
    row = iota((rows, index.shape[1]), 0) == (index >> 8)
    for ch in range(CH):
        part = slice(ch * rows, (ch + 1) * rows)
        found = mm(high_ref[part, :], column) + mm(low_ref[part, :], column)
        out_ref[0, ch : ch + 1, :] = jnp.sum(jnp.where(row, found, 0.0), axis=0, keepdims=True)


def render_kernel(
    length_ref, own_ref, rank_ref, reply_ref, target_ref, image_ref, out_ref,
    vals, grads, falloff_ref, trans_ref, high_ref, low_ref, shade_ref, before_ref,
):
    tile = pl.program_id(0)
    devices = reply_ref.shape[0] // CH
    cap = reply_ref.shape[1]
    slots = own_ref.shape[2]
    pixels = target_ref.shape[2]
    blocks = slots // SB
    length = length_ref[tile]
    mine = iota((devices, slots), 0) == own_ref[0]
    places = one_hot(rank_ref[0], cap)
    reply_high, reply_low = split(reply_ref[...])
    vals[...] = jnp.zeros_like(vals)
    live = jnp.where(iota((1, slots), 1) < length, 1.0, 0.0)
    for ch in range(CH):
        part = slice(ch * devices, (ch + 1) * devices)
        found = mm(reply_high[part], places) + mm(reply_low[part], places)
        value = jnp.sum(jnp.where(mine, found, 0.0), axis=0, keepdims=True)
        if ch == 5:
            value = value * live
        row = ch if ch < 6 else ch + 2
        vals[row : row + 1, :] = value

    strict = jnp.where(iota((SB, SB), 0) < iota((SB, SB), 1), 1.0, 0.0).astype(BF16)
    inclusive = jnp.where(iota((SB, SB), 0) <= iota((SB, SB), 1), 1.0, 0.0).astype(BF16)
    centres = iota((SIDE, SB), 0).astype(F32) + 0.5
    side_rows = pixels // SIDE

    carry = jnp.zeros((pixels, 1), F32)
    image = jnp.zeros((8, pixels), F32)
    for blk in range(blocks):
        at = slice(blk * SB, (blk + 1) * SB)
        dx = centres - vals[0:1, at]
        dy = centres - vals[1:2, at]
        ex = 0.5 * vals[2:3, at] * dx * dx
        ey = 0.5 * vals[4:5, at] * dy * dy
        bdy = vals[3:4, at] * dy
        opacity = vals[5:6, at]
        for y in range(side_rows):
            rows = slice(y * SIDE, (y + 1) * SIDE)
            exponent = ex + ey[y : y + 1] + dx * bdy[y : y + 1]
            falloff = jnp.exp(-exponent)
            falloff_ref[rows, at] = falloff
            keep = jnp.log(1.0 - opacity * falloff)
            high, low = split(keep)
            high_ref[rows, :] = high
            low_ref[rows, :] = low
        total = mm(high_ref[...], strict) + mm(low_ref[...], strict) + carry
        last = high_ref[:, SB - 128 :].astype(F32) + low_ref[:, SB - 128 :].astype(F32)
        carry = total[:, SB - 1 : SB] + last[:, 127:128]
        trans = jnp.exp(total)
        trans_ref[:, at] = trans
        weight_high, weight_low = split(trans * (opacity * falloff_ref[:, at]))
        colour_high, colour_low = split(vals[8:16, at])
        image = image + (
            mm_nt(colour_high, weight_high)
            + mm_nt(colour_low, weight_high)
            + mm_nt(colour_high, weight_low)
        )
    image_ref[0] = image
    grad_image = 2.0 * (image - target_ref[0])
    grand_total = jnp.sum(grad_image * image, axis=0, keepdims=True)
    grand_total = jnp.transpose(jnp.broadcast_to(grand_total, (128, pixels)))
    grand_total = jnp.concatenate([grand_total] * (SB // 128), axis=1)
    grad_high, grad_low = split(grad_image)
    turned_high, turned_low = split(jnp.transpose(grad_image))

    spent = jnp.zeros((pixels, 1), F32)
    for blk in range(blocks):
        at = slice(blk * SB, (blk + 1) * SB)
        mean_x, mean_y = vals[0:1, at], vals[1:2, at]
        conic_a, conic_b, conic_c = vals[2:3, at], vals[3:4, at], vals[4:5, at]
        opacity = vals[5:6, at]
        dx = centres - mean_x
        dy = centres - mean_y
        colour_high, colour_low = split(vals[8:16, at])
        shading = (
            mm(turned_high, colour_high) + mm(turned_high, colour_low) + mm(turned_low, colour_high)
        )
        shade_ref[...] = shading
        weight = trans_ref[:, at] * (opacity * falloff_ref[:, at])
        weight_high, weight_low = split(weight)
        grads[8:16, at] = (
            mm(grad_high, weight_high) + mm(grad_low, weight_high) + mm(grad_high, weight_low)
        )
        high, low = split(weight * shading)
        before = mm(high, inclusive) + mm(low, inclusive) + spent
        spent = before[:, SB - 1 : SB]
        before_ref[...] = grand_total - before
        power0 = jnp.zeros((SIDE, SB), F32)
        power1 = power0
        power2 = power0
        opaque = power0
        for y in range(side_rows):
            rows = slice(y * SIDE, (y + 1) * SIDE)
            falloff = falloff_ref[rows, at]
            alpha = opacity * falloff
            grad_alpha = trans_ref[rows, at] * shade_ref[rows, :] - before_ref[rows, :] / (
                1.0 - alpha
            )
            opaque = opaque + grad_alpha * falloff
            power = grad_alpha * alpha
            power0 = power0 - power
            moment = power * dy[y : y + 1]
            power1 = power1 - moment
            power2 = power2 - moment * dy[y : y + 1]
        across = power0 * dx
        sum_x = jnp.sum(across, axis=0, keepdims=True)
        sum_y = jnp.sum(power1, axis=0, keepdims=True)
        grads[0:1, at] = -(conic_a * sum_x + conic_b * sum_y)
        grads[1:2, at] = -(conic_c * sum_y + conic_b * sum_x)
        grads[2:3, at] = 0.5 * jnp.sum(across * dx, axis=0, keepdims=True)
        grads[3:4, at] = jnp.sum(power1 * dx, axis=0, keepdims=True)
        grads[4:5, at] = 0.5 * jnp.sum(power2, axis=0, keepdims=True)
        grads[5:6, at] = jnp.sum(opaque, axis=0, keepdims=True) * live[:, at]

    for ch in range(CH):
        part = slice(ch * devices, (ch + 1) * devices)
        row = ch if ch < 6 else ch + 2
        high, low = split(jnp.where(mine, grads[row : row + 1, :], 0.0))
        sent = mm_nt(high, places) + mm_nt(low, places)

        @pl.when(tile == 0)
        def _():
            out_ref[part, :] = sent

        @pl.when(tile > 0)
        def _():
            out_ref[part, :] += sent


def scatter_kernel(ask_ref, grad_ref, out_ref, row_ref, column_ref):
    rows, width = out_ref.shape[1], out_ref.shape[2]
    count = ask_ref.shape[1]
    step = min(1024, count)

    @pl.when(pl.program_id(0) == 0)
    def _():
        def build(j, none):
            at = pl.ds(pl.multiple_of(j * step, step), step)
            index = ask_ref[:, at]
            row_ref[:, at] = one_hot(index >> 8, rows)
            column_ref[:, at] = one_hot(index & (width - 1), width)
            return none

        lax.fori_loop(0, count // step, build, 0)

    total = jnp.zeros((rows, width), F32)

    def add(j, total):
        at = pl.ds(pl.multiple_of(j * step, step), step)
        grad = jnp.broadcast_to(grad_ref[0, :, at], (16, step))
        high, low = split(grad)
        tops = row_ref[:, at]
        column = column_ref[:, at]
        left_high = jnp.concatenate([tops[k : k + 16] * high for k in range(0, rows, 16)], axis=0)
        left_low = jnp.concatenate([tops[k : k + 16] * low for k in range(0, rows, 16)], axis=0)
        return total + (mm_nt(left_high, column) + mm_nt(left_low, column))

    out_ref[0] = lax.fori_loop(0, count // step, add, total)


def body(splat_params, list_owner, list_slot, list_length, target):
    devices = lax.axis_size(("row", "col"))
    tiles, slots = list_slot.shape
    entries = tiles * slots
    splats = splat_params.shape[1]
    pixels = target.shape[2]
    cap = 2 * entries // devices
    total = devices * cap
    width = 256
    rows = splats // width
    owners = list_owner.reshape(1, entries)
    requests, ranks = pl.pallas_call(
        plan_kernel,
        out_shape=(
            jax.ShapeDtypeStruct((devices, cap), jnp.int32),
            jax.ShapeDtypeStruct((1, entries), jnp.int32),
        ),
        name="plan",
    )(owners, list_slot.reshape(1, entries))
    asked = lax.all_to_all(requests, ("row", "col"), split_axis=0, concat_axis=0, tiled=True)
    steps = total // LANES
    table = splat_params.reshape(CH * rows, width)
    looked = pl.pallas_call(
        gather_kernel,
        grid=(steps,),
        in_specs=[
            pl.BlockSpec((1, 1, LANES), lambda i: (i, 0, 0)),
            pl.BlockSpec((CH * rows, width), lambda i: (0, 0)),
        ],
        out_specs=pl.BlockSpec((1, CH, LANES), lambda i: (i, 0, 0)),
        out_shape=jax.ShapeDtypeStruct((steps, CH, LANES), F32),
        scratch_shapes=[
            pltpu.VMEM((CH * rows, width), BF16),
            pltpu.VMEM((CH * rows, width), BF16),
        ],
        name="lookup",
    )(asked.reshape(steps, 1, LANES), table)
    per = LANES // cap
    looked = looked.reshape(steps, CH, per, cap).transpose(0, 2, 1, 3).reshape(devices, CH, cap)
    answer = lax.all_to_all(looked, ("row", "col"), split_axis=0, concat_axis=0, tiled=True)
    replies = answer.transpose(1, 0, 2).reshape(CH * devices, cap)
    targets = jnp.pad(target.transpose(1, 0, 2), ((0, 0), (0, 4), (0, 0)))
    images, outgoing = pl.pallas_call(
        render_kernel,
        grid=(tiles,),
        in_specs=[
            pl.BlockSpec(memory_space=pltpu.SMEM),
            pl.BlockSpec((1, 1, slots), lambda i: (i, 0, 0)),
            pl.BlockSpec((1, 1, slots), lambda i: (i, 0, 0)),
            pl.BlockSpec((CH * devices, cap), lambda i: (0, 0)),
            pl.BlockSpec((1, 8, pixels), lambda i: (i, 0, 0)),
        ],
        out_specs=(
            pl.BlockSpec((1, 8, pixels), lambda i: (i, 0, 0)),
            pl.BlockSpec((CH * devices, cap), lambda i: (0, 0)),
        ),
        out_shape=(
            jax.ShapeDtypeStruct((tiles, 8, pixels), F32),
            jax.ShapeDtypeStruct((CH * devices, cap), F32),
        ),
        scratch_shapes=[
            pltpu.VMEM((16, slots), F32),
            pltpu.VMEM((16, slots), F32),
            pltpu.VMEM((pixels, slots), F32),
            pltpu.VMEM((pixels, slots), F32),
            pltpu.VMEM((pixels, SB), BF16),
            pltpu.VMEM((pixels, SB), BF16),
            pltpu.VMEM((pixels, SB), F32),
            pltpu.VMEM((pixels, SB), F32),
        ],
        name="render",
    )(
        list_length,
        owners.reshape(tiles, 1, slots),
        ranks.reshape(tiles, 1, slots),
        replies,
        targets,
    )
    rendered = images[:, :4].transpose(1, 0, 2)
    sending = outgoing.reshape(CH, devices, cap).transpose(1, 0, 2)
    incoming = lax.all_to_all(sending, ("row", "col"), split_axis=0, concat_axis=0, tiled=True)
    arrived = incoming.transpose(1, 0, 2).reshape(CH, 1, total)
    splat_grads = pl.pallas_call(
        scatter_kernel,
        grid=(CH,),
        in_specs=[
            pl.BlockSpec((1, total), lambda i: (0, 0)),
            pl.BlockSpec((1, 1, total), lambda i: (i, 0, 0)),
        ],
        out_specs=pl.BlockSpec((1, rows, width), lambda i: (i, 0, 0)),
        out_shape=jax.ShapeDtypeStruct((CH, rows, width), F32),
        scratch_shapes=[
            pltpu.VMEM((rows, total), BF16),
            pltpu.VMEM((width, total), BF16),
        ],
        name="accumulate",
    )(asked.reshape(1, total), arrived)
    return (rendered, splat_grads.reshape(CH, splats))


def solution(mesh):
    in_specs = (
        P(None, ("row", "col")),
        P(("row", "col"), None, None),
        P(("row", "col"), None),
        P(("row", "col")),
        P(None, ("row", "col"), None),
    )
    out_specs = (P(None, ("row", "col"), None), P(None, ("row", "col")))
    return jax.shard_map(body, mesh=mesh, in_specs=in_specs, out_specs=out_specs, check_vma=False)
```

time: 440 us -> 193 us (0.44)
  local copies, waits for them, and re-layouts: 226 us -> 19.4 us
  Pallas kernels: 0 us -> 126 us
  other arithmetic: 102 us -> 0 us
  matrix products: 38.7 us -> 0 us
  blocking collectives: 33.6 us -> 0 us
  waiting for transfers between devices: 15.4 us -> 32.9 us
  loops' own time: 4.77 us -> 0 us
    pallas_call x0 -> x4, Pallas kernels: none -> 126 us  [the longest x1 48 us: body(): pl.pallas_call(render_kernel, grid=(tiles,), in_specs=[pl.BlockSpec(memor...]
    gather x19 -> x0, local copies, waits for them, and re-layouts: 119 us -> none  [the longest x1 44 us: body(): fetched = replies[:, owners, slot_rank].reshape(10, tile_count, list_count)]
    scatter-add x1 -> x0, other arithmetic: 63.9 us -> none  [body(): jnp.zeros(splat_params.shape, jnp.float32).at[:, asked_slots[0]]]
    unnamed x19 -> x9, local copies, waits for them, and re-layouts: 65.5 us -> 9.14 us
    dot_general x72 -> x0, matrix products: 38.7 us -> none  [the longest x12 10.4 us: backward(): jnp.dot(spent_sum, inclusive, precision=precise)]
    all_to_all x1 -> x0, blocking collectives: 33.6 us -> none  [body(): lax.all_to_all(outgoing, ('row', 'col'), split_axis=1, concat_axis=1, til...]
    scatter x2 -> x0, local copies, waits for them, and re-layouts: 18.4 us -> none  [the longest x1 15.5 us: body(): slot_rank = jnp.zeros((entries,), jnp.int32).at[sort_order].set(position)]
    sub x1 -> x0, other arithmetic: 15.9 us -> none  [body(): position = jnp.arange(entries, dtype=jnp.int32) - starts[sorted_owner]]
  transfers between devices with their start and end apart: 2 -> 3, of which waited for: 1 -> 3; matrix products, arithmetic and copies ran while one was open for 4% -> 3% of each run, Pallas kernels for 0% -> 0%
where the time goes in v1:
time: 193 us; the launch traced here: 192 us
  Pallas kernels  126 us (65%)
  waiting for transfers between devices  32.9 us (17%)
  local copies, waits for them, and re-layouts  19.4 us (10%)
  starting transfers between devices  13 us (7%)
    pallas_call x1, Pallas kernels, body(): pl.pallas_call(render_kernel, grid=(tiles,), in_specs=[pl.BlockSpec(memor...  48 us
    pallas_call x1, Pallas kernels, body(): pl.pallas_call(scatter_kernel, grid=(CH,), in_specs=[pl.BlockSpec((1, tot...  41.9 us
    pallas_call x1, Pallas kernels, body(): pl.pallas_call(gather_kernel, grid=(steps,), in_specs=[pl.BlockSpec((1, 1...  31.2 us
    all_to_all x1, waiting for transfers between devices, body(): lax.all_to_all(looked, ('row', 'col'), split_axis=0, concat_axis=0, tiled...  15 us
    all_to_all x1, waiting for transfers between devices, body(): lax.all_to_all(sending, ('row', 'col'), split_axis=0, concat_axis=0, tile...  14.1 us
    unnamed x9, local copies, waits for them, and re-layouts  9.14 us
    all_to_all x1, starting transfers between devices, body(): lax.all_to_all(requests, ('row', 'col'), split_axis=0, concat_axis=0, til...  7.33 us
    pallas_call x1, Pallas kernels, body(): pl.pallas_call(plan_kernel, out_shape=(jax.ShapeDtypeStruct((devices, cap...  5.2 us
  transfers between devices with their start and end apart: 3, of which 3 were waited for; matrix products, arithmetic and copies ran while one was open for 3% of the time, Pallas kernels for 0%

profile of v1, /device:TPU:0, one launch (start us, length us, event | category | flops | bytes accessed | tf_op | source)
XLA Modules:
  0.0 192.3 jit_solution(8482088278354218159)
XLA Ops:
  0.6 1.3 copy.15
  2.0 5.2 %plan.1 = (s32[32,256]{1,0:T(8,128)}, s32[1,4096]{1,0:T(1,128)}) custom-call(s32[1,4096]{1,0:T(1,128)} %bitcast.29, s32[1,4096]{1,0:T(1,128)} %bitcast.32), custom_call_target="tpu_custom_call" | custom-call | tf_op jit(solution)/shard_map/plan/pallas_call | solution.py:260
  7.2 1.4 all_to_all.12
  8.6 7.3 %all-to-all-start = ((s32[32,1,256]{2,1,0:T(1,128)}), s32[32,1,256]{2,1,0:T(1,128)S(1)}, u32[]{:S(2)}, u32[]{:S(2)}) async-start(s32[32,1,256]{2,1,0:T(1,128)} %all_to_all.12), calls=%async_computation | async-start | bytes 65536 | tf_op jit(solution)/shard_map/all_to_all | solution.py:268
  15.9 0.0 copy-start.1
  15.9 3.4 %reshape.39.table_ref = f32[2560,256]{1,0:T(8,128)} reshape(f32[10,65536]{1,0:T(8,128)} %param.5) | data formatting | bytes 5242880 | tf_op jit(solution)/shard_map/reshape | solution.py:270
  19.3 3.8 %all-to-all-done.ask_ref = s32[32,1,256]{2,1,0:T(1,128)S(1)} async-done(((s32[32,1,256]{2,1,0:T(1,128)}), s32[32,1,256]{2,1,0:T(1,128)S(1)}, u32[]{:S(2)}, u32[]{:S(2)}) %all-to-all-start) | async-done | bytes 32800 | tf_op jit(solution)/shard_map/all_to_all | solution.py:268
  23.1 0.6 copy-done
  23.8 31.2 %lookup.1 = f32[32,10,256]{2,1,0:T(8,128)} custom-call(s32[32,1,256]{2,1,0:T(1,128)} %copy-done, f32[2560,256]{1,0:T(8,128)} %reshape.39.table_ref), custom_call_target="tpu_custom_call" | custom-call | tf_op jit(solution)/shard_map/lookup/pallas_call | solution.py:271
  54.9 2.6 %all-to-all-start.1 = ((f32[32,10,256]{2,1,0:T(8,128)}), f32[32,10,256]{2,1,0:T(8,128)S(1)}, u32[]{:S(2)}, u32[]{:S(2)}) async-start(f32[32,10,256]{2,1,0:T(8,128)} %lookup.1), calls=%async_computation.1 | async-start | bytes 1048576 | tf_op jit(solution)/shard_map/all_to_all | solution.py:288
  57.6 0.6 pad.4.target_ref
  58.2 15.0 %all-to-all-done.1 = f32[32,10,256]{2,1,0:T(8,128)S(1)} async-done(((f32[32,10,256]{2,1,0:T(8,128)}), f32[32,10,256]{2,1,0:T(8,128)S(1)}, u32[]{:S(2)}, u32[]{:S(2)}) %all-to-all-start.1) | async-done | bytes 327712 | tf_op jit(solution)/shard_map/all_to_all | solution.py:288
  73.2 0.9 copy.10
  74.1 48.0 %render.1 = (f32[4,8,256]{2,1,0:T(8,128)}, f32[320,256]{1,0:T(8,128)}) custom-call(s32[4]{0:T(128)} %length_ref.1, s32[4,1,1024]{2,1,0:T(1,128)} %bitcast.30, s32[4,1,1024]{2,1,0:T(1,128)} %bitcast.33, f32[320,256]{1,0:T(8,128)} %bitcast.26, f32[4,8,256]{2,1,0:T(8,128)} %pad.4.target_ref), custom_call_target="tpu_custom_call" | custom-call | tf_op jit(solution)/shard_map/render/pallas_call | solution.py:291
  122.1 2.0 %copy.19 = f32[10,32,256]{2,0,1:T(8,128)} copy(f32[10,32,256]{2,1,0:T(8,128)} %bitcast.27) | data formatting | bytes 655360 | tf_op jit(solution)/shard_map/reshape | solution.py:328
  124.1 3.1 %all-to-all-start.2 = ((f32[32,10,256]{2,1,0:T(8,128)}), f32[32,10,256]{2,1,0:T(8,128)S(1)}, u32[]{:S(2)}, u32[]{:S(2)}) async-start(f32[32,10,256]{2,1,0:T(8,128)} %bitcast.20), calls=%async_computation.2 | async-start | bytes 1048576 | tf_op jit(solution)/shard_map/all_to_all | solution.py:329
  127.1 0.8 slice_bitcast_fusion
  127.9 0.6 copy.14
  128.5 14.1 %all-to-all-done.2 = f32[32,10,256]{2,1,0:T(8,128)S(1)} async-done(((f32[32,10,256]{2,1,0:T(8,128)}), f32[32,10,256]{2,1,0:T(8,128)S(1)}, u32[]{:S(2)}, u32[]{:S(2)}) %all-to-all-start.2) | async-done | bytes 327712 | tf_op jit(solution)/shard_map/all_to_all | solution.py:329
  142.6 0.2 copy.13
  142.8 1.0 reshape.43.grad_ref
  143.8 41.9 %accumulate.1 = f32[10,256,256]{2,1,0:T(8,128)} custom-call(s32[1,8192]{1,0:T(1,128)} %bitcast.28, f32[10,1,8192]{2,1,0:T(1,128)} %reshape.43.grad_ref), custom_call_target="tpu_custom_call" | custom-call | tf_op jit(solution)/shard_map/accumulate/pallas_call | solution.py:331
  185.7 2.1 %pad.5 = f32[16,256,256]{2,1,0:T(8,128)S(1)} pad(f32[10,256,256]{2,1,0:T(8,128)} %accumulate.1, f32[]{:T(128)} %constant.2.clone.1), padding=0_6x0_0x0_0 | pad | bytes 6815748
  187.8 4.4 %copy.16 = f32[2,8,256,256]{3,1,2,0:T(8,128)} copy(f32[2,8,256,256]{3,2,1,0:T(8,128)S(1)} %bitcast.22) | data formatting | bytes 8388608
  (3 shorter events, 0.0 us)
Async XLA Ops:
  8.6 14.6 %all-to-all-start = ((s32[32,1,256]{2,1,0:T(1,128)}), s32[32,1,256]{2,1,0:T(1,128)S(1)}, u32[]{:S(2)}, u32[]{:S(2)}) async-start(s32[32,1,256]{2,1,0:T(1,128)} %all_to_all.12), calls=%async_computation | async-start | bytes 65536 | tf_op jit(solution)/shard_map/all_to_all | solution.py:268
  15.9 41.6 %copy-start.1 = (f32[4,4,256]{2,1,0:T(4,128)S(1)}, f32[4,4,256]{2,1,0:T(4,128)}, u32[]{:S(2)}) copy-start(f32[4,4,256]{2,1,0:T(4,128)} %param.9) | copy-start | bytes 49156
  23.1 0.6 copy-start
  54.9 18.2 %all-to-all-start.1 = ((f32[32,10,256]{2,1,0:T(8,128)}), f32[32,10,256]{2,1,0:T(8,128)S(1)}, u32[]{:S(2)}, u32[]{:S(2)}) async-start(f32[32,10,256]{2,1,0:T(8,128)} %lookup.1), calls=%async_computation.1 | async-start | bytes 1048576 | tf_op jit(solution)/shard_map/all_to_all | solution.py:288
  124.1 18.5 %all-to-all-start.2 = ((f32[32,10,256]{2,1,0:T(8,128)}), f32[32,10,256]{2,1,0:T(8,128)S(1)}, u32[]{:S(2)}, u32[]{:S(2)}) async-start(f32[32,10,256]{2,1,0:T(8,128)} %bitcast.20), calls=%async_computation.2 | async-start | bytes 1048576 | tf_op jit(solution)/shard_map/all_to_all | solution.py:329

commit v2 on v1

--- a/solution.py
+++ b/solution.py
@@ -61,7 +61,7 @@
     req_ref[...] = (high * 256.0 + low).astype(jnp.int32)
 
 
-def gather_kernel(ask_ref, table_ref, out_ref, high_ref, low_ref):
+def gather_kernel(ask_ref, table_ref, out_ref, parts_ref):
     width = table_ref.shape[1]
     rows = table_ref.shape[0] // CH
 
@@ -70,21 +70,21 @@
         for ch in range(CH):
             part = slice(ch * rows, (ch + 1) * rows)
             high, low = split(table_ref[part, :])
-            high_ref[part, :] = high
-            low_ref[part, :] = low
+            parts_ref[part, :width] = high
+            parts_ref[part, width:] = low
 
     index = ask_ref[0]
     column = one_hot(index & (width - 1), width)
     row = iota((rows, index.shape[1]), 0) == (index >> 8)
+    found = mm(parts_ref[...], jnp.concatenate([column, column], axis=0))
     for ch in range(CH):
-        part = slice(ch * rows, (ch + 1) * rows)
-        found = mm(high_ref[part, :], column) + mm(low_ref[part, :], column)
-        out_ref[0, ch : ch + 1, :] = jnp.sum(jnp.where(row, found, 0.0), axis=0, keepdims=True)
+        picked = jnp.where(row, found[ch * rows : (ch + 1) * rows], 0.0)
+        out_ref[0, ch : ch + 1, :] = jnp.sum(picked, axis=0, keepdims=True)
 
 
 def render_kernel(
     length_ref, own_ref, rank_ref, reply_ref, target_ref, image_ref, out_ref,
-    vals, grads, falloff_ref, trans_ref, high_ref, low_ref, shade_ref, before_ref,
+    vals, grads, falloff_ref, trans_ref, high_ref, low_ref, shade_ref, before_ref, pack_ref,
 ):
     tile = pl.program_id(0)
     devices = reply_ref.shape[0] // CH
@@ -96,12 +96,12 @@
     mine = iota((devices, slots), 0) == own_ref[0]
     places = one_hot(rank_ref[0], cap)
     reply_high, reply_low = split(reply_ref[...])
+    fetched = mm(reply_high, places) + mm(reply_low, places)
     vals[...] = jnp.zeros_like(vals)
     live = jnp.where(iota((1, slots), 1) < length, 1.0, 0.0)
     for ch in range(CH):
         part = slice(ch * devices, (ch + 1) * devices)
-        found = mm(reply_high[part], places) + mm(reply_low[part], places)
-        value = jnp.sum(jnp.where(mine, found, 0.0), axis=0, keepdims=True)
+        value = jnp.sum(jnp.where(mine, fetched[part], 0.0), axis=0, keepdims=True)
         if ch == 5:
             value = value * live
         row = ch if ch < 6 else ch + 2
@@ -113,7 +113,7 @@
     side_rows = pixels // SIDE
 
     carry = jnp.zeros((pixels, 1), F32)
-    image = jnp.zeros((8, pixels), F32)
+    image = jnp.zeros((pixels, 8), F32)
     for blk in range(blocks):
         at = slice(blk * SB, (blk + 1) * SB)
         dx = centres - vals[0:1, at]
@@ -139,17 +139,19 @@
         weight_high, weight_low = split(trans * (opacity * falloff_ref[:, at]))
         colour_high, colour_low = split(vals[8:16, at])
         image = image + (
-            mm_nt(colour_high, weight_high)
-            + mm_nt(colour_low, weight_high)
-            + mm_nt(colour_high, weight_low)
+            mm_nt(weight_high, colour_high)
+            + mm_nt(weight_high, colour_low)
+            + mm_nt(weight_low, colour_high)
         )
-    image_ref[0] = image
-    grad_image = 2.0 * (image - target_ref[0])
-    grand_total = jnp.sum(grad_image * image, axis=0, keepdims=True)
-    grand_total = jnp.transpose(jnp.broadcast_to(grand_total, (128, pixels)))
-    grand_total = jnp.concatenate([grand_total] * (SB // 128), axis=1)
+    rendered = jnp.transpose(image)
+    image_ref[0] = rendered
+    grad_image = 2.0 * (rendered - target_ref[0])
     grad_high, grad_low = split(grad_image)
-    turned_high, turned_low = split(jnp.transpose(grad_image))
+    grad_wide = grad_high.astype(F32)
+    grad_rest = grad_image - grad_wide
+    turned = jnp.transpose(jnp.concatenate([grad_wide, grad_wide, grad_rest, grad_image], axis=0))
+    turned_parts = turned.astype(BF16)
+    grand_total = jnp.sum(jnp.transpose(grad_image) * image, axis=1, keepdims=True)
 
     spent = jnp.zeros((pixels, 1), F32)
     for blk in range(blocks):
@@ -159,10 +161,12 @@
         opacity = vals[5:6, at]
         dx = centres - mean_x
         dy = centres - mean_y
-        colour_high, colour_low = split(vals[8:16, at])
-        shading = (
-            mm(turned_high, colour_high) + mm(turned_high, colour_low) + mm(turned_low, colour_high)
-        )
+        colours = vals[8:16, at]
+        colour_wide = colours.astype(BF16).astype(F32)
+        colour_parts = jnp.concatenate(
+            [colour_wide, colours - colour_wide, colour_wide, jnp.zeros_like(colours)], axis=0
+        ).astype(BF16)
+        shading = mm(turned_parts, colour_parts)
         shade_ref[...] = shading
         weight = trans_ref[:, at] * (opacity * falloff_ref[:, at])
         weight_high, weight_low = split(weight)
@@ -204,46 +208,53 @@
         part = slice(ch * devices, (ch + 1) * devices)
         row = ch if ch < 6 else ch + 2
         high, low = split(jnp.where(mine, grads[row : row + 1, :], 0.0))
-        sent = mm_nt(high, places) + mm_nt(low, places)
-
-        @pl.when(tile == 0)
-        def _():
-            out_ref[part, :] = sent
-
-        @pl.when(tile > 0)
-        def _():
-            out_ref[part, :] += sent
-
-
-def scatter_kernel(ask_ref, grad_ref, out_ref, row_ref, column_ref):
-    rows, width = out_ref.shape[1], out_ref.shape[2]
-    count = ask_ref.shape[1]
-    step = min(1024, count)
-
-    @pl.when(pl.program_id(0) == 0)
-    def _():
-        def build(j, none):
-            at = pl.ds(pl.multiple_of(j * step, step), step)
-            index = ask_ref[:, at]
-            row_ref[:, at] = one_hot(index >> 8, rows)
-            column_ref[:, at] = one_hot(index & (width - 1), width)
-            return none
-
-        lax.fori_loop(0, count // step, build, 0)
-
-    total = jnp.zeros((rows, width), F32)
-
-    def add(j, total):
-        at = pl.ds(pl.multiple_of(j * step, step), step)
-        grad = jnp.broadcast_to(grad_ref[0, :, at], (16, step))
+        pack_ref[0, part, :] = high
+        pack_ref[1, part, :] = low
+    sent = mm_nt(pack_ref[0], places) + mm_nt(pack_ref[1], places)
+
+    @pl.when(tile == 0)
+    def _():
+        out_ref[...] = sent
+
+    @pl.when(tile > 0)
+    def _():
+        out_ref[...] += sent
+
+
+def scatter_kernel(ask_ref, grad_ref, out_ref, high_ref, low_ref, sum_ref):
+    step = pl.program_id(0)
+    halves = sum_ref.shape[0]
+    width = halves * 128
+    rows = sum_ref.shape[1] // CH
+    index = ask_ref[...]
+    column = one_hot(index & (width - 1), width)
+    tops = one_hot(index >> 8, rows)
+    for ch in range(CH):
+        grad = jnp.broadcast_to(grad_ref[ch : ch + 1, :], (16, index.shape[1]))
         high, low = split(grad)
-        tops = row_ref[:, at]
-        column = column_ref[:, at]
-        left_high = jnp.concatenate([tops[k : k + 16] * high for k in range(0, rows, 16)], axis=0)
-        left_low = jnp.concatenate([tops[k : k + 16] * low for k in range(0, rows, 16)], axis=0)
-        return total + (mm_nt(left_high, column) + mm_nt(left_low, column))
-
-    out_ref[0] = lax.fori_loop(0, count // step, add, total)
+        for k in range(0, rows, 16):
+            part = slice(ch * rows + k, ch * rows + k + 16)
+            high_ref[part, :] = tops[k : k + 16] * high
+            low_ref[part, :] = tops[k : k + 16] * low
+    total = mm_nt(high_ref[...], column) + mm_nt(low_ref[...], column)
+
+    @pl.when(step == 0)
+    def _():
+        for k in range(halves):
+            sum_ref[k] = total[:, k * 128 : (k + 1) * 128]
+
+    @pl.when(step > 0)
+    def _():
+        for k in range(halves):
+            sum_ref[k] += total[:, k * 128 : (k + 1) * 128]
+
+    @pl.when(step == pl.num_programs(0) - 1)
+    def _():
+        for q in range(rows):
+            for k in range(halves):
+                at = slice((q * halves + k) * 128, (q * halves + k + 1) * 128)
+                out_ref[0:8, at] = sum_ref[k, pl.ds(q, 8, stride=rows), :]
+                out_ref[8:CH, at] = sum_ref[k, pl.ds(8 * rows + q, CH - 8, stride=rows), :]
 
 
 def body(splat_params, list_owner, list_slot, list_length, target):
@@ -278,8 +289,7 @@
         out_specs=pl.BlockSpec((1, CH, LANES), lambda i: (i, 0, 0)),
         out_shape=jax.ShapeDtypeStruct((steps, CH, LANES), F32),
         scratch_shapes=[
-            pltpu.VMEM((CH * rows, width), BF16),
-            pltpu.VMEM((CH * rows, width), BF16),
+            pltpu.VMEM((CH * rows, 2 * width), BF16),
         ],
         name="lookup",
     )(asked.reshape(steps, 1, LANES), table)
@@ -315,6 +325,7 @@
             pltpu.VMEM((pixels, SB), BF16),
             pltpu.VMEM((pixels, SB), F32),
             pltpu.VMEM((pixels, SB), F32),
+            pltpu.VMEM((2, CH * devices, slots), BF16),
         ],
         name="render",
     )(
@@ -327,23 +338,25 @@
     rendered = images[:, :4].transpose(1, 0, 2)
     sending = outgoing.reshape(CH, devices, cap).transpose(1, 0, 2)
     incoming = lax.all_to_all(sending, ("row", "col"), split_axis=0, concat_axis=0, tiled=True)
-    arrived = incoming.transpose(1, 0, 2).reshape(CH, 1, total)
+    arrived = incoming.transpose(1, 0, 2).reshape(CH, total)
+    chunk = min(512, total)
     splat_grads = pl.pallas_call(
         scatter_kernel,
-        grid=(CH,),
+        grid=(total // chunk,),
         in_specs=[
-            pl.BlockSpec((1, total), lambda i: (0, 0)),
-            pl.BlockSpec((1, 1, total), lambda i: (i, 0, 0)),
-        ],
-        out_specs=pl.BlockSpec((1, rows, width), lambda i: (i, 0, 0)),
-        out_shape=jax.ShapeDtypeStruct((CH, rows, width), F32),
+            pl.BlockSpec((1, chunk), lambda i: (0, i)),
+            pl.BlockSpec((CH, chunk), lambda i: (0, i)),
+        ],
+        out_specs=pl.BlockSpec((CH, splats), lambda i: (0, 0)),
+        out_shape=jax.ShapeDtypeStruct((CH, splats), F32),
         scratch_shapes=[
-            pltpu.VMEM((rows, total), BF16),
-            pltpu.VMEM((width, total), BF16),
+            pltpu.VMEM((CH * rows, chunk), BF16),
+            pltpu.VMEM((CH * rows, chunk), BF16),
+            pltpu.VMEM((width // 128, CH * rows, 128), F32),
         ],
         name="accumulate",
     )(asked.reshape(1, total), arrived)
-    return (rendered, splat_grads.reshape(CH, splats))
+    return (rendered, splat_grads)
 
 
 def solution(mesh):

time: 193 us -> 150 us (0.78)
  Pallas kernels: 126 us -> 89.4 us
  local copies, waits for them, and re-layouts: 19.4 us -> 12.9 us
    pallas_call x1, Pallas kernels: 48 us -> 19.5 us  [body(): pl.pallas_call(render_kernel, grid=(tiles,), in_specs=[pl.BlockSpec(memor...]
    pallas_call x1, Pallas kernels: 41.9 us -> 33.7 us  [body(): pl.pallas_call(scatter_kernel, grid=(total // chunk,), in_specs=[pl.Block...]
    unnamed x9, local copies, waits for them, and re-layouts: 9.14 us -> 3.72 us
  transfers between devices with their start and end apart: 3 -> 3, of which waited for: 3 -> 3; matrix products, arithmetic and copies ran while one was open for 3% -> 4% of each run, Pallas kernels for 0% -> 0%
where the time goes in v2:
time: 150 us; the launch traced here: 149 us
  Pallas kernels  89.4 us (60%)
  waiting for transfers between devices  32.9 us (22%)
  starting transfers between devices  13 us (9%)
  local copies, waits for them, and re-layouts  12.9 us (9%)
    pallas_call x1, Pallas kernels, body(): pl.pallas_call(scatter_kernel, grid=(total // chunk,), in_specs=[pl.Block...  33.7 us
    pallas_call x1, Pallas kernels, body(): pl.pallas_call(gather_kernel, grid=(steps,), in_specs=[pl.BlockSpec((1, 1...  31.1 us
    pallas_call x1, Pallas kernels, body(): pl.pallas_call(render_kernel, grid=(tiles,), in_specs=[pl.BlockSpec(memor...  19.5 us
    all_to_all x1, waiting for transfers between devices, body(): lax.all_to_all(looked, ('row', 'col'), split_axis=0, concat_axis=0, tiled...  15 us
    all_to_all x1, waiting for transfers between devices, body(): lax.all_to_all(sending, ('row', 'col'), split_axis=0, concat_axis=0, tile...  14.1 us
    all_to_all x1, starting transfers between devices, body(): lax.all_to_all(requests, ('row', 'col'), split_axis=0, concat_axis=0, til...  7.33 us
    pallas_call x1, Pallas kernels, body(): pl.pallas_call(plan_kernel, out_shape=(jax.ShapeDtypeStruct((devices, cap...  5.2 us
    all_to_all x1, waiting for transfers between devices, body(): lax.all_to_all(requests, ('row', 'col'), split_axis=0, concat_axis=0, til...  3.85 us
  transfers between devices with their start and end apart: 3, of which 3 were waited for; matrix products, arithmetic and copies ran while one was open for 4% of the time, Pallas kernels for 0%

profile of v2, /device:TPU:0, one launch (start us, length us, event | category | flops | bytes accessed | tf_op | source)
XLA Modules:
  0.0 149.0 jit_solution(3478984865124809436)
XLA Ops:
  0.6 1.3 copy.15
  2.0 5.2 %plan.1 = (s32[32,256]{1,0:T(8,128)}, s32[1,4096]{1,0:T(1,128)}) custom-call(s32[1,4096]{1,0:T(1,128)} %bitcast.29, s32[1,4096]{1,0:T(1,128)} %bitcast.32), custom_call_target="tpu_custom_call" | custom-call | tf_op jit(solution)/shard_map/plan/pallas_call | solution.py:271
  7.2 1.4 all_to_all.12
  8.6 7.3 %all-to-all-start = ((s32[32,1,256]{2,1,0:T(1,128)}), s32[32,1,256]{2,1,0:T(1,128)S(1)}, u32[]{:S(2)}, u32[]{:S(2)}) async-start(s32[32,1,256]{2,1,0:T(1,128)} %all_to_all.12), calls=%async_computation | async-start | bytes 65536 | tf_op jit(solution)/shard_map/all_to_all | solution.py:279
  15.9 0.0 copy-start.1
  15.9 3.4 %reshape.36.table_ref = f32[2560,256]{1,0:T(8,128)} reshape(f32[10,65536]{1,0:T(8,128)} %param.5) | data formatting | bytes 5242880 | tf_op jit(solution)/shard_map/reshape | solution.py:281
  19.3 3.8 %all-to-all-done.ask_ref = s32[32,1,256]{2,1,0:T(1,128)S(1)} async-done(((s32[32,1,256]{2,1,0:T(1,128)}), s32[32,1,256]{2,1,0:T(1,128)S(1)}, u32[]{:S(2)}, u32[]{:S(2)}) %all-to-all-start) | async-done | bytes 32800 | tf_op jit(solution)/shard_map/all_to_all | solution.py:279
  23.1 0.0 copy-start
  23.1 0.6 copy-done
  23.8 31.1 %lookup.1 = f32[32,10,256]{2,1,0:T(8,128)} custom-call(s32[32,1,256]{2,1,0:T(1,128)} %copy-done, f32[2560,256]{1,0:T(8,128)} %reshape.36.table_ref), custom_call_target="tpu_custom_call" | custom-call | tf_op jit(solution)/shard_map/lookup/pallas_call | solution.py:282
  54.9 2.6 %all-to-all-start.1 = ((f32[32,10,256]{2,1,0:T(8,128)}), f32[32,10,256]{2,1,0:T(8,128)S(1)}, u32[]{:S(2)}, u32[]{:S(2)}) async-start(f32[32,10,256]{2,1,0:T(8,128)} %lookup.1), calls=%async_computation.1 | async-start | bytes 1048576 | tf_op jit(solution)/shard_map/all_to_all | solution.py:298
  57.5 0.0 copy-done.1
  57.5 0.6 pad.4.target_ref
  58.1 15.0 %all-to-all-done.1 = f32[32,10,256]{2,1,0:T(8,128)S(1)} async-done(((f32[32,10,256]{2,1,0:T(8,128)}), f32[32,10,256]{2,1,0:T(8,128)S(1)}, u32[]{:S(2)}, u32[]{:S(2)}) %all-to-all-start.1) | async-done | bytes 327712 | tf_op jit(solution)/shard_map/all_to_all | solution.py:298
  73.1 0.9 copy.10
  74.0 19.5 %render.1 = (f32[4,8,256]{2,1,0:T(8,128)}, f32[320,256]{1,0:T(8,128)}) custom-call(s32[4]{0:T(128)} %length_ref.1, s32[4,1,1024]{2,1,0:T(1,128)} %bitcast.30, s32[4,1,1024]{2,1,0:T(1,128)} %bitcast.33, f32[320,256]{1,0:T(8,128)} %bitcast.26, f32[4,8,256]{2,1,0:T(8,128)} %pad.4.target_ref), custom_call_target="tpu_custom_call" | custom-call | tf_op jit(solution)/shard_map/render/pallas_call | solution.py:301
  93.5 2.0 %copy.19 = f32[10,32,256]{2,0,1:T(8,128)} copy(f32[10,32,256]{2,1,0:T(8,128)} %bitcast.27) | data formatting | bytes 655360 | tf_op jit(solution)/shard_map/reshape | solution.py:339
  95.5 3.1 %all-to-all-start.2 = ((f32[32,10,256]{2,1,0:T(8,128)}), f32[32,10,256]{2,1,0:T(8,128)S(1)}, u32[]{:S(2)}, u32[]{:S(2)}) async-start(f32[32,10,256]{2,1,0:T(8,128)} %bitcast.20), calls=%async_computation.2 | async-start | bytes 1048576 | tf_op jit(solution)/shard_map/all_to_all | solution.py:340
  98.5 0.8 slice_bitcast_fusion
  99.3 0.6 copy.14
  99.9 14.1 %all-to-all-done.2 = f32[32,10,256]{2,1,0:T(8,128)S(1)} async-done(((f32[32,10,256]{2,1,0:T(8,128)}), f32[32,10,256]{2,1,0:T(8,128)S(1)}, u32[]{:S(2)}, u32[]{:S(2)}) %all-to-all-start.2) | async-done | bytes 327712 | tf_op jit(solution)/shard_map/all_to_all | solution.py:340
  114.0 0.2 copy.13
  114.2 1.1 copy.16
  115.3 33.7 %accumulate.1 = f32[10,65536]{1,0:T(8,128)} custom-call(s32[1,8192]{1,0:T(1,128)} %bitcast.28, f32[10,8192]{1,0:T(8,128)} %bitcast.22), custom_call_target="tpu_custom_call" | custom-call | tf_op jit(solution)/shard_map/accumulate/pallas_call | solution.py:343
  (2 shorter events, 0.0 us)
Async XLA Ops:
  8.6 14.6 %all-to-all-start = ((s32[32,1,256]{2,1,0:T(1,128)}), s32[32,1,256]{2,1,0:T(1,128)S(1)}, u32[]{:S(2)}, u32[]{:S(2)}) async-start(s32[32,1,256]{2,1,0:T(1,128)} %all_to_all.12), calls=%async_computation | async-start | bytes 65536 | tf_op jit(solution)/shard_map/all_to_all | solution.py:279
  15.9 41.6 %copy-start.1 = (f32[4,4,256]{2,1,0:T(4,128)S(1)}, f32[4,4,256]{2,1,0:T(4,128)}, u32[]{:S(2)}) copy-start(f32[4,4,256]{2,1,0:T(4,128)} %param.9) | copy-start | bytes 49156
  23.1 0.6 copy-start
  54.9 18.2 %all-to-all-start.1 = ((f32[32,10,256]{2,1,0:T(8,128)}), f32[32,10,256]{2,1,0:T(8,128)S(1)}, u32[]{:S(2)}, u32[]{:S(2)}) async-start(f32[32,10,256]{2,1,0:T(8,128)} %lookup.1), calls=%async_computation.1 | async-start | bytes 1048576 | tf_op jit(solution)/shard_map/all_to_all | solution.py:298
  95.5 18.5 %all-to-all-start.2 = ((f32[32,10,256]{2,1,0:T(8,128)}), f32[32,10,256]{2,1,0:T(8,128)S(1)}, u32[]{:S(2)}, u32[]{:S(2)}) async-start(f32[32,10,256]{2,1,0:T(8,128)} %bitcast.20), calls=%async_computation.2 | async-start | bytes 1048576 | tf_op jit(solution)/shard_map/all_to_all | solution.py:340

commit v3 on v2

--- a/solution.py
+++ b/solution.py
@@ -11,6 +11,8 @@
 SB = 256
 LANES = 256
 CH = 10
+EARLY = 6
+TOP = 8
 F32 = jnp.float32
 BF16 = jnp.bfloat16
 NT = (((1,), (1,)), ((), ()))
@@ -63,11 +65,12 @@
 
 def gather_kernel(ask_ref, table_ref, out_ref, parts_ref):
     width = table_ref.shape[1]
-    rows = table_ref.shape[0] // CH
+    channels = out_ref.shape[1]
+    rows = table_ref.shape[0] // channels
 
     @pl.when(pl.program_id(0) == 0)
     def _():
-        for ch in range(CH):
+        for ch in range(channels):
             part = slice(ch * rows, (ch + 1) * rows)
             high, low = split(table_ref[part, :])
             parts_ref[part, :width] = high
@@ -77,7 +80,7 @@
     column = one_hot(index & (width - 1), width)
     row = iota((rows, index.shape[1]), 0) == (index >> 8)
     found = mm(parts_ref[...], jnp.concatenate([column, column], axis=0))
-    for ch in range(CH):
+    for ch in range(channels):
         picked = jnp.where(row, found[ch * rows : (ch + 1) * rows], 0.0)
         out_ref[0, ch : ch + 1, :] = jnp.sum(picked, axis=0, keepdims=True)
 
@@ -221,15 +224,17 @@
         out_ref[...] += sent
 
 
-def scatter_kernel(ask_ref, grad_ref, out_ref, high_ref, low_ref, sum_ref):
+def scatter_kernel(ask_ref, grad_ref, *refs):
+    out_ref, high_ref, low_ref, sum_ref = refs[-4:]
+    channels = grad_ref.shape[0]
     step = pl.program_id(0)
     halves = sum_ref.shape[0]
     width = halves * 128
-    rows = sum_ref.shape[1] // CH
+    rows = sum_ref.shape[1] // channels
     index = ask_ref[...]
     column = one_hot(index & (width - 1), width)
     tops = one_hot(index >> 8, rows)
-    for ch in range(CH):
+    for ch in range(channels):
         grad = jnp.broadcast_to(grad_ref[ch : ch + 1, :], (16, index.shape[1]))
         high, low = split(grad)
         for k in range(0, rows, 16):
@@ -253,8 +258,7 @@
         for q in range(rows):
             for k in range(halves):
                 at = slice((q * halves + k) * 128, (q * halves + k + 1) * 128)
-                out_ref[0:8, at] = sum_ref[k, pl.ds(q, 8, stride=rows), :]
-                out_ref[8:CH, at] = sum_ref[k, pl.ds(8 * rows + q, CH - 8, stride=rows), :]
+                out_ref[0:channels, at] = sum_ref[k, pl.ds(q, channels, stride=rows), :]
 
 
 def body(splat_params, list_owner, list_slot, list_length, target):
@@ -278,24 +282,39 @@
     )(owners, list_slot.reshape(1, entries))
     asked = lax.all_to_all(requests, ("row", "col"), split_axis=0, concat_axis=0, tiled=True)
     steps = total // LANES
-    table = splat_params.reshape(CH * rows, width)
-    looked = pl.pallas_call(
-        gather_kernel,
-        grid=(steps,),
-        in_specs=[
-            pl.BlockSpec((1, 1, LANES), lambda i: (i, 0, 0)),
-            pl.BlockSpec((CH * rows, width), lambda i: (0, 0)),
-        ],
-        out_specs=pl.BlockSpec((1, CH, LANES), lambda i: (i, 0, 0)),
-        out_shape=jax.ShapeDtypeStruct((steps, CH, LANES), F32),
-        scratch_shapes=[
-            pltpu.VMEM((CH * rows, 2 * width), BF16),
-        ],
-        name="lookup",
-    )(asked.reshape(steps, 1, LANES), table)
     per = LANES // cap
-    looked = looked.reshape(steps, CH, per, cap).transpose(0, 2, 1, 3).reshape(devices, CH, cap)
-    answer = lax.all_to_all(looked, ("row", "col"), split_axis=0, concat_axis=0, tiled=True)
+
+    def lookup(params, asked):
+        channels = params.shape[0]
+        table = params.reshape(channels * rows, width)
+        looked = pl.pallas_call(
+            gather_kernel,
+            grid=(steps,),
+            in_specs=[
+                pl.BlockSpec((1, 1, LANES), lambda i: (i, 0, 0)),
+                pl.BlockSpec((channels * rows, width), lambda i: (0, 0)),
+            ],
+            out_specs=pl.BlockSpec((1, channels, LANES), lambda i: (i, 0, 0)),
+            out_shape=jax.ShapeDtypeStruct((steps, channels, LANES), F32),
+            scratch_shapes=[pltpu.VMEM((channels * rows, 2 * width), BF16)],
+            cost_estimate=pl.CostEstimate(
+                flops=4 * channels * splats * total,
+                bytes_accessed=4 * channels * (splats + total),
+                transcendentals=0,
+            ),
+            name="lookup",
+        )(asked.reshape(steps, 1, LANES), table)
+        looked = looked.reshape(steps, channels, per, cap).transpose(0, 2, 1, 3)
+        return looked.reshape(devices, channels, cap)
+
+    def exchange(values):
+        return lax.all_to_all(values, ("row", "col"), split_axis=0, concat_axis=0, tiled=True)
+
+    first = lookup(splat_params[:EARLY], asked)
+    first, asked = lax.optimization_barrier((first, asked))
+    first_answer = exchange(first)
+    second_answer = exchange(lookup(splat_params[EARLY:], asked))
+    answer = jnp.concatenate([first_answer, second_answer], axis=1)
     replies = answer.transpose(1, 0, 2).reshape(CH * devices, cap)
     targets = jnp.pad(target.transpose(1, 0, 2), ((0, 0), (0, 4), (0, 0)))
     images, outgoing = pl.pallas_call(
@@ -336,26 +355,40 @@
         targets,
     )
     rendered = images[:, :4].transpose(1, 0, 2)
-    sending = outgoing.reshape(CH, devices, cap).transpose(1, 0, 2)
-    incoming = lax.all_to_all(sending, ("row", "col"), split_axis=0, concat_axis=0, tiled=True)
-    arrived = incoming.transpose(1, 0, 2).reshape(CH, total)
+    outgoing = outgoing.reshape(CH, devices, cap)
     chunk = min(512, total)
-    splat_grads = pl.pallas_call(
-        scatter_kernel,
-        grid=(total // chunk,),
-        in_specs=[
-            pl.BlockSpec((1, chunk), lambda i: (0, i)),
-            pl.BlockSpec((CH, chunk), lambda i: (0, i)),
-        ],
-        out_specs=pl.BlockSpec((CH, splats), lambda i: (0, 0)),
-        out_shape=jax.ShapeDtypeStruct((CH, splats), F32),
-        scratch_shapes=[
-            pltpu.VMEM((CH * rows, chunk), BF16),
-            pltpu.VMEM((CH * rows, chunk), BF16),
-            pltpu.VMEM((width // 128, CH * rows, 128), F32),
-        ],
-        name="accumulate",
-    )(asked.reshape(1, total), arrived)
+
+    def accumulate(incoming, block, held):
+        channels = incoming.shape[1]
+        arrived = incoming.transpose(1, 0, 2).reshape(channels, total)
+        return pl.pallas_call(
+            scatter_kernel,
+            grid=(total // chunk,),
+            in_specs=[
+                pl.BlockSpec((1, chunk), lambda i: (0, i)),
+                pl.BlockSpec((channels, chunk), lambda i: (0, i)),
+            ]
+            + [pl.BlockSpec(memory_space=pl.ANY)] * len(held),
+            out_specs=pl.BlockSpec((TOP, splats), lambda i: (block, 0)),
+            out_shape=jax.ShapeDtypeStruct((CH, splats), F32),
+            scratch_shapes=[
+                pltpu.VMEM((channels * rows, chunk), BF16),
+                pltpu.VMEM((channels * rows, chunk), BF16),
+                pltpu.VMEM((width // 128, channels * rows, 128), F32),
+            ],
+            input_output_aliases={2: 0} if held else {},
+            cost_estimate=pl.CostEstimate(
+                flops=4 * channels * splats * total,
+                bytes_accessed=4 * channels * (splats + total),
+                transcendentals=0,
+            ),
+            name="accumulate",
+        )(asked.reshape(1, total), arrived, *held)
+
+    rest = exchange(outgoing[TOP:].transpose(1, 0, 2))
+    main = exchange(outgoing[:TOP].transpose(1, 0, 2))
+    held = accumulate(rest, 1, ())
+    splat_grads = accumulate(main, 0, (held,))
     return (rendered, splat_grads)
 
 

time: 150 us -> 172 us (1.15)
  Pallas kernels: 89.4 us -> 107 us
  waiting for transfers between devices: 32.9 us -> 15.9 us
  blocking collectives: 0 us -> 13 us
  local copies, waits for them, and re-layouts: 12.9 us -> 17.8 us
  starting transfers between devices: 13 us -> 15.2 us
    pallas_call x2 -> x4, Pallas kernels: 64.8 us -> 81.9 us  [the longest x2 42.4 us: lookup(): pl.pallas_call(gather_kernel, grid=(steps,), in_specs=[pl.BlockSpec((1, 1...]
    all_to_all x2 -> x3, waiting for transfers between devices: 29 us -> 14.9 us  [exchange(): lax.all_to_all(values, ('row', 'col'), split_axis=0, concat_axis=0, tiled...]
    all_to_all x0 -> x1, blocking collectives: none -> 13 us  [exchange(): lax.all_to_all(values, ('row', 'col'), split_axis=0, concat_axis=0, tiled...]
    slice x0 -> x7, local copies, waits for them, and re-layouts: none -> 5.93 us  [the longest x1 2.57 us: body(): second_answer = exchange(lookup(splat_params[EARLY:], asked))]
    all_to_all x1, waiting for transfers between devices: 3.85 us -> 1.01 us  [body(): lax.all_to_all(requests, ('row', 'col'), split_axis=0, concat_axis=0, til...]
    all_to_all x2 -> x3, starting transfers between devices: 5.66 us -> 7.92 us  [exchange(): lax.all_to_all(values, ('row', 'col'), split_axis=0, concat_axis=0, tiled...]
    reshape x2 -> x3, local copies, waits for them, and re-layouts: 5.36 us -> 4.27 us  [the longest x2 3.65 us: lookup(): table = params.reshape(channels * rows, width)]
    unnamed x9 -> x13, local copies, waits for them, and re-layouts: 3.72 us -> 3.9 us
  transfers between devices with their start and end apart: 3 -> 4, of which waited for: 3 -> 3; matrix products, arithmetic and copies ran while one was open for 4% -> 6% of each run, Pallas kernels for 0% -> 7%
where the time goes in v3:
time: 172 us; the launch traced here: 169 us
  Pallas kernels  107 us (62%)
  local copies, waits for them, and re-layouts  17.8 us (10%)
  waiting for transfers between devices  15.9 us (9%)
  starting transfers between devices  15.2 us (9%)
  blocking collectives  13 us (8%)
    pallas_call x2, Pallas kernels, lookup(): pl.pallas_call(gather_kernel, grid=(steps,), in_specs=[pl.BlockSpec((1, 1...  42.4 us
    pallas_call x2, Pallas kernels, accumulate(): pl.pallas_call(scatter_kernel, grid=(total // chunk,), in_specs=[pl.Block...  39.5 us
    pallas_call x1, Pallas kernels, body(): pl.pallas_call(render_kernel, grid=(tiles,), in_specs=[pl.BlockSpec(memor...  19.5 us
    all_to_all x3, waiting for transfers between devices, exchange(): lax.all_to_all(values, ('row', 'col'), split_axis=0, concat_axis=0, tiled...  14.9 us
    all_to_all x1, blocking collectives, exchange(): lax.all_to_all(values, ('row', 'col'), split_axis=0, concat_axis=0, tiled...  13 us
    all_to_all x3, starting transfers between devices, exchange(): lax.all_to_all(values, ('row', 'col'), split_axis=0, concat_axis=0, tiled...  7.92 us
    all_to_all x1, starting transfers between devices, body(): lax.all_to_all(requests, ('row', 'col'), split_axis=0, concat_axis=0, til...  7.33 us
    pallas_call x1, Pallas kernels, body(): pl.pallas_call(plan_kernel, out_shape=(jax.ShapeDtypeStruct((devices, cap...  5.2 us
  transfers between devices with their start and end apart: 4, of which 3 were waited for; matrix products, arithmetic and copies ran while one was open for 6% of the time, Pallas kernels for 7%

profile of v3, /device:TPU:0, one launch (start us, length us, event | category | flops | bytes accessed | tf_op | source)
XLA Modules:
  0.0 169.3 jit_solution(7769991223025377345)
XLA Ops:
  0.6 1.3 copy.20
  2.0 5.2 %plan.1 = (s32[32,256]{1,0:T(8,128)}, s32[1,4096]{1,0:T(1,128)}) custom-call(s32[1,4096]{1,0:T(1,128)} %bitcast.41, s32[1,4096]{1,0:T(1,128)} %bitcast.45), custom_call_target="tpu_custom_call" | custom-call | tf_op jit(solution)/shard_map/plan/pallas_call | solution.py:275
  7.2 1.4 copy.13
  8.6 7.3 %all-to-all-start = ((s32[32,1,256]{2,1,0:T(1,128)}), s32[32,1,256]{2,1,0:T(1,128)S(1)}, u32[]{:S(2)}, u32[]{:S(2)}) async-start(s32[32,1,256]{2,1,0:T(1,128)} %copy.13), calls=%async_computation | async-start | bytes 65536 | tf_op jit(solution)/shard_map/all_to_all | solution.py:283
  15.9 2.6 %slice.22 = f32[4,65536]{1,0:T(4,128)S(1)} slice(f32[10,65536]{1,0:T(8,128)} %param.5), slice={[6:10], [0:65536]} | slice | bytes 2097152 | tf_op jit(solution)/shard_map/slice | solution.py:316
  18.5 1.7 %reshape.47.table_ref = f32[1024,256]{1,0:T(8,128)} reshape(f32[4,65536]{1,0:T(4,128)S(1)} %slice.22) | data formatting | bytes 2097152 | tf_op jit(solution)/shard_map/reshape | solution.py:289
  20.2 2.0 %reshape.45.table_ref = f32[1536,256]{1,0:T(8,128)} reshape(f32[6,65536]{1,0:T(8,128)S(1)} %slice-done) | data formatting | bytes 3145728 | tf_op jit(solution)/shard_map/reshape | solution.py:289
  22.1 1.0 all-to-all-done.ask_ref
  23.7 22.4 %lookup.2 = f32[32,6,256]{2,1,0:T(8,128)} custom-call(s32[32,1,256]{2,1,0:T(1,128)} %copy-done.1, f32[1536,256]{1,0:T(8,128)} %reshape.45.table_ref), custom_call_target="tpu_custom_call" | custom-call | flops 12884901888 | bytes 1769472 | tf_op jit(solution)/shard_map/lookup/pallas_call | solution.py:290
  46.7 20.0 %lookup.3 = f32[32,4,256]{2,1,0:T(4,128)} custom-call(s32[32,1,256]{2,1,0:T(1,128)} %reshape.46.ask_ref, f32[1024,256]{1,0:T(8,128)} %reshape.47.table_ref), custom_call_target="tpu_custom_call" | custom-call | flops 8589934592 | bytes 1179648 | tf_op jit(solution)/shard_map/lookup/pallas_call | solution.py:290
  66.8 13.0 %all_to_all.32 = f32[32,4,256]{2,1,0:T(4,128)S(1)} all-to-all(f32[32,4,256]{2,1,0:T(4,128)} %lookup.3), channel_id=1, replica_groups=mesh['row'=4,'col'=8] {'row','col'}, dimensions={0} | all-to-all | bytes 262144 | tf_op jit(solution)/shard_map/all_to_all | solution.py:311
  79.8 2.6 %all-to-all-start.1 = ((f32[32,6,256]{2,1,0:T(8,128)}), f32[32,6,256]{2,1,0:T(8,128)S(1)}, u32[]{:S(2)}, u32[]{:S(2)}) async-start(f32[32,6,256]{2,1,0:T(8,128)} %lookup.2), calls=%async_computation.1 | async-start | bytes 524288 | tf_op jit(solution)/shard_map/all_to_all | solution.py:311
  83.0 9.9 %all-to-all-done.1 = f32[32,6,256]{2,1,0:T(8,128)S(1)} async-done(((f32[32,6,256]{2,1,0:T(8,128)}), f32[32,6,256]{2,1,0:T(8,128)S(1)}, u32[]{:S(2)}, u32[]{:S(2)}) %all-to-all-start.1) | async-done | bytes 196640 | tf_op jit(solution)/shard_map/all_to_all | solution.py:311
  93.0 0.9 copy.14
  94.0 19.5 %render.1 = (f32[4,8,256]{2,1,0:T(8,128)}, f32[320,256]{1,0:T(8,128)}) custom-call(s32[4]{0:T(128)} %length_ref.1, s32[4,1,1024]{2,1,0:T(1,128)} %bitcast.42, s32[4,1,1024]{2,1,0:T(1,128)} %bitcast.49, f32[320,256]{1,0:T(8,128)} %bitcast.35, f32[4,8,256]{2,1,0:T(8,128)} %pad.4.target_ref), custom_call_target="tpu_custom_call" | custom-call | tf_op jit(solution)/shard_map/render/pallas_call | solution.py:320
  113.4 0.8 slice.26
  115.0 2.6 %all-to-all-start.4 = ((f32[32,2,256]{2,1,0:T(2,128)}), f32[32,2,256]{2,1,0:T(2,128)S(1)}, u32[]{:S(2)}, u32[]{:S(2)}) async-start(f32[32,2,256]{2,1,0:T(2,128)} %bitcast.32), calls=%async_computation.4 | async-start | bytes 131072 | tf_op jit(solution)/shard_map/all_to_all | solution.py:311
  118.2 1.0 slice.24
  119.1 0.9 copy.26
  120.0 4.9 %all-to-all-done.4 = f32[32,2,256]{2,1,0:T(2,128)S(1)} async-done(((f32[32,2,256]{2,1,0:T(2,128)}), f32[32,2,256]{2,1,0:T(2,128)S(1)}, u32[]{:S(2)}, u32[]{:S(2)}) %all-to-all-start.4) | async-done | bytes 65568 | tf_op jit(solution)/shard_map/all_to_all | solution.py:311
  124.9 2.8 %all-to-all-start.3 = ((f32[32,8,256]{2,1,0:T(8,128)}), f32[32,8,256]{2,1,0:T(8,128)S(1)}, u32[]{:S(2)}, u32[]{:S(2)}) async-start(f32[32,8,256]{2,1,0:T(8,128)} %bitcast.31), calls=%async_computation.3 | async-start | bytes 524288 | tf_op jit(solution)/shard_map/all_to_all | solution.py:311
  127.7 0.8 slice_bitcast_fusion
  129.1 12.1 %accumulate.2.refs_0_ = f32[10,65536]{1,0:T(8,128)} custom-call(s32[1,8192]{1,0:T(1,128)} %bitcast.46, f32[2,8192]{1,0:T(2,128)} %bitcast.44), custom_call_target="tpu_custom_call" | custom-call | flops 4294967296 | bytes 589824 | tf_op jit(solution)/shard_map/accumulate/pallas_call | solution.py:364
  141.9 27.5 %accumulate.3 = f32[10,65536]{1,0:T(8,128)} custom-call(s32[1,8192]{1,0:T(1,128)} %bitcast.47, f32[8,8192]{1,0:T(8,128)} %bitcast.39, f32[10,65536]{1,0:T(8,128)} %accumulate.2.refs_0_), custom_call_target="tpu_custom_call", output_to_operand_aliasing={{}: (2, {})} | custom-call | flops 17179869184 | bytes 2359296 | tf_op jit(solution)/shard_map/accumulate/pallas_call | solution.py:364
  (19 shorter events, 4.5 us)
Async XLA Ops:
  8.6 14.6 %all-to-all-start = ((s32[32,1,256]{2,1,0:T(1,128)}), s32[32,1,256]{2,1,0:T(1,128)S(1)}, u32[]{:S(2)}, u32[]{:S(2)}) async-start(s32[32,1,256]{2,1,0:T(1,128)} %copy.13), calls=%async_computation | async-start | bytes 65536 | tf_op jit(solution)/shard_map/all_to_all | solution.py:283
  15.9 4.3 %slice-start = ((f32[10,65536]{1,0:T(8,128)}), f32[6,65536]{1,0:T(8,128)S(1)}, s32[]{:S(2)}) async-start(f32[10,65536]{1,0:T(8,128)} %param.5), calls=%async_computation.5 | async-start | bytes 4194304 | tf_op jit(solution)/shard_map/slice | solution.py:313
  23.1 0.6 copy-start.1
  46.7 35.7 %copy-start.3 = (f32[4,4,256]{2,1,0:T(4,128)S(1)}, f32[4,4,256]{2,1,0:T(4,128)}, u32[]{:S(2)}) copy-start(f32[4,4,256]{2,1,0:T(4,128)} %param.9) | copy-start | bytes 49156
  79.8 13.2 %all-to-all-start.1 = ((f32[32,6,256]{2,1,0:T(8,128)}), f32[32,6,256]{2,1,0:T(8,128)S(1)}, u32[]{:S(2)}, u32[]{:S(2)}) async-start(f32[32,6,256]{2,1,0:T(8,128)} %lookup.2), calls=%async_computation.1 | async-start | bytes 524288 | tf_op jit(solution)/shard_map/all_to_all | solution.py:311
  115.0 10.0 %all-to-all-start.4 = ((f32[32,2,256]{2,1,0:T(2,128)}), f32[32,2,256]{2,1,0:T(2,128)S(1)}, u32[]{:S(2)}, u32[]{:S(2)}) async-start(f32[32,2,256]{2,1,0:T(2,128)} %bitcast.32), calls=%async_computation.4 | async-start | bytes 131072 | tf_op jit(solution)/shard_map/all_to_all | solution.py:311
  124.9 4.1 %copy-start.2 = (f32[32,2,256]{2,1,0:T(2,128)}, f32[32,2,256]{2,1,0:T(2,128)S(1)}, u32[]{:S(2)}) copy-start(f32[32,2,256]{2,1,0:T(2,128)S(1)} %all-to-all-done.4) | copy-start | bytes 196612
  124.9 16.2 %all-to-all-start.3 = ((f32[32,8,256]{2,1,0:T(8,128)}), f32[32,8,256]{2,1,0:T(8,128)S(1)}, u32[]{:S(2)}, u32[]{:S(2)}) async-start(f32[32,8,256]{2,1,0:T(8,128)} %bitcast.31), calls=%async_computation.3 | async-start | bytes 524288 | tf_op jit(solution)/shard_map/all_to_all | solution.py:311
  141.2 0.7 copy-start
